TPU v7x, 256 devices: a whole 4x4x8 slice. The times are simulated.
256 devices in a mesh: ep: 32 (over z, y), tp: 8 (over x, core).
Axes of the slice: x: 4, y: 4, z: 8, core: 2. Of those that a mesh axis runs over, the one named last changes fastest.
Arguments:
- tokens: bfloat16 [1024, 6144], P('ep', 'tp'), may hold values from -6 to 6
- expert_ids: int32 [1024, 2], P('ep'), may hold values from 0 to 7, all different within a row; in each aligned block of 32 rows (0 to 31, 32 to 63, ...) at most 16 rows name the same one
- combine_weights: float32 [1024, 2], P('ep'), may hold values from 0.1 to 1
- gate_codes: bfloat16 [6144, 65536], P(None, ('ep', 'tp')), may hold values from -6 to 6, as said below
- gate_scales: bfloat16 [192, 65536], P(None, ('ep', 'tp')), as said below
- up_codes: bfloat16 [6144, 65536], P(None, ('ep', 'tp')), may hold values from -6 to 6, as said below
- up_scales: bfloat16 [192, 65536], P(None, ('ep', 'tp')), as said below
- down_codes: bfloat16 [65536, 6144], P(('ep', 'tp')), may hold values from -6 to 6, as said below
- down_scales: bfloat16 [2048, 6144], P(('ep', 'tp')), as said below
Outputs:
- mixed: bfloat16 [1024, 6144], P('ep', 'tp')
Inputs may be any that keep to these rules, and one draw needn't show every extreme that they name: `expert_ids`: each token names 2 different experts. Among the 32 tokens of one index of ep no expert is named more than 16 times, a bound that some block reaches. `gate_codes`: every entry is one of 0, 0.5, 1, 1.5, 2, 3, 4, 6 or its negative. `up_codes`: every entry is one of 0, 0.5, 1, 1.5, 2, 3, 4, 6 or its negative. `down_codes`: every entry is one of 0, 0.5, 1, 1.5, 2, 3, 4, 6 or its negative. `gate_scales`: every entry is a power of two. `up_scales`: every entry is a power of two. `down_scales`: every entry is a power of two.
All inputs are finite; a program needn't handle non-finite values.
Results may differ from a plain program's by a relative error of at most 0.014.
Values may be sent and summed in bfloat16 or wider, within the bound.
A program may use at most 128 MiB of HBM per device.

v0:
```python
import jax
import jax.numpy as jnp
from jax import lax
from jax.sharding import PartitionSpec as P

EXPERTS = 8
CAP = 16


def dequant(code_values, scales):
    count_in, count_out = code_values.shape
    blocks = code_values.reshape(count_in // 32, 32, count_out) * scales[:, None, :]
    return blocks.reshape(count_in, count_out)


def slot_targets(expert_ids):
    count_tokens, count_top = expert_ids.shape
    flat_ids = expert_ids.reshape(-1)
    is_expert = (flat_ids[:, None] == jnp.arange(EXPERTS, dtype=jnp.int32)[None, :]).astype(
        jnp.int32
    )
    before = jnp.cumsum(is_expert, axis=0) - is_expert
    slot_rank = jnp.sum(before * is_expert, axis=1)
    return (flat_ids * CAP + slot_rank).reshape(count_tokens, count_top)


def per_device(
    tokens,
    expert_ids,
    combine_weights,
    gate_codes,
    gate_scales,
    up_codes,
    up_scales,
    down_codes,
    down_scales,
):
    owners = lax.axis_size("ep") // EXPERTS
    gate_matrix = dequant(gate_codes, gate_scales)
    up_matrix = dequant(up_codes, up_scales)
    down_matrix = dequant(down_codes, down_scales)
    target = slot_targets(expert_ids)
    slot_index = jnp.arange(EXPERTS * CAP, dtype=jnp.int32)
    chosen = jnp.zeros((EXPERTS * CAP, target.shape[0]), jnp.float32)
    weighting = jnp.zeros((target.shape[0], EXPERTS * CAP), jnp.float32)
    for column in range(target.shape[1]):
        match_rows = target[:, column][:, None] == slot_index[None, :]
        weighting = weighting + combine_weights[:, column][:, None] * match_rows.astype(jnp.float32)
        chosen = chosen + jnp.transpose(match_rows).astype(jnp.float32)
    chosen = chosen.astype(jnp.bfloat16)
    packed = jnp.dot(chosen, tokens, preferred_element_type=jnp.float32).astype(jnp.bfloat16)
    packed = packed.reshape(EXPERTS, CAP, tokens.shape[1])
    slot_rows = lax.all_gather(
        lax.all_to_all(
            jnp.repeat(packed, owners, axis=0), "ep", split_axis=0, concat_axis=0, tiled=True
        ),
        "tp",
        axis=2,
        tiled=True,
    )
    count_src, count_slots, model_width = slot_rows.shape
    flat_rows = slot_rows.reshape(count_src * count_slots, model_width)
    gate_proj = jnp.dot(flat_rows, gate_matrix, preferred_element_type=jnp.float32)
    up_proj = jnp.dot(flat_rows, up_matrix, preferred_element_type=jnp.float32)
    hidden = (jax.nn.silu(gate_proj) * up_proj).astype(jnp.bfloat16)
    partial_value = jnp.dot(hidden, down_matrix, preferred_element_type=jnp.float32).astype(
        jnp.bfloat16
    )
    partial_value = partial_value.reshape(count_src, count_slots, model_width)
    reduced = lax.psum_scatter(
        partial_value.astype(jnp.float32).astype(jnp.bfloat16),
        "tp",
        scatter_dimension=2,
        tiled=True,
    ).astype(jnp.float32)
    returned = lax.all_to_all(
        reduced.astype(jnp.bfloat16), "ep", split_axis=0, concat_axis=0, tiled=True
    ).astype(reduced.dtype)
    feature_width = returned.shape[2]
    grouped = returned.reshape(EXPERTS, owners, CAP, feature_width)
    per_expert = jnp.sum(grouped, axis=1).reshape(EXPERTS * CAP, feature_width)
    mixed_out = jnp.dot(weighting, per_expert, preferred_element_type=jnp.float32)
    return mixed_out.astype(jnp.bfloat16)


def solution(mesh):
    placed = (
        P("ep", "tp"),
        P("ep", None),
        P("ep", None),
        P(None, ("ep", "tp")),
        P(None, ("ep", "tp")),
        P(None, ("ep", "tp")),
        P(None, ("ep", "tp")),
        P(("ep", "tp"), None),
        P(("ep", "tp"), None),
    )
    return jax.shard_map(
        per_device, mesh=mesh, in_specs=placed, out_specs=P("ep", "tp"), check_vma=False
    )
```

profile of v0, /device:TPU:8, one launch (start us, length us, event | category | flops | bytes accessed | tf_op | source)
XLA Modules:
  0.0 188.0 jit_solution(12755171529070535130)
XLA Ops:
  6.5 0.0 copy-start
  6.5 0.0 copy-start.1
  6.5 0.0 copy-start.4
  6.5 0.0 all-gather.2.cloned.1.call-start
  6.5 0.9 copy.16
  7.5 0.1 eq.59
  7.6 0.1 fusion.9
  7.6 0.1 reduce_window_sum.11
  7.7 0.2 select_reduce_fusion
  7.9 0.1 reduce_sum.21
  8.0 0.1 copy.17
  8.1 0.7 multiply_add_fusion
  8.8 0.0 copy-done
  8.8 0.2 convolution_convert_fusion.1
  9.0 0.1 broadcast_in_dim.2
  9.1 34.1 %all_to_all.10 = bf16[32,16,768]{2,1,0:T(8,128)(2,1)} all-to-all(bf16[32,16,768]{2,1,0:T(8,128)(2,1)S(1)} %bitcast.30), channel_id=1, replica_groups=mesh['ep'=32,'tp'=8] {'ep'}, dimensions={0} | all-to-all | bytes 1572864 | tf_op jit(solution)/shard_map/all_to_all | solution.py:54
  43.1 0.0 all-gather.2.cloned.1.call-update
  43.2 0.0 copy-start.5
  43.2 0.0 reduce-scatter.2.cloned.1.call-start
  43.2 0.0 copy-done.1
  43.2 0.0 copy-done.4
  43.2 0.0 copy-start.2
  43.2 1.9 %bitcast_multiply_fusion.2 = bf16[6144,256]{1,0:T(8,128)(2,1)} fusion(bf16[6144,256]{1,0:T(8,128)(2,1)S(1)} %copy-done.1, bf16[192,256]{1,0:T(8,128)(2,1)S(1)} %copy-done.4), kind=kLoop, calls=%fused_computation.3 | loop fusion | flops 1572864 | bytes 6389760 | tf_op jit(solution)/shard_map/mul | solution.py:12
  45.2 0.0 copy-done.5
  45.2 1.1 copy-done.2
  46.3 0.0 copy-start.3
  46.3 0.0 copy-start.6
  46.3 0.3 bitcast_multiply_fusion
  46.6 1.6 copy-done.3
  48.2 0.0 copy-done.6
  48.2 1.9 %bitcast_multiply_fusion.1 = bf16[6144,256]{1,0:T(8,128)(2,1)} fusion(bf16[6144,256]{1,0:T(8,128)(2,1)S(1)} %copy-done.3, bf16[192,256]{1,0:T(8,128)(2,1)S(1)} %copy-done.6), kind=kLoop, calls=%fused_computation.2 | loop fusion | flops 1572864 | bytes 6389760 | tf_op jit(solution)/shard_map/mul | solution.py:12
  50.1 33.4 %all-gather.2.cloned.1.call-done = bf16[32,16,6144]{2,1,0:T(8,128)(2,1)} async-done(((bf16[32,16,768]{2,1,0:T(8,128)(2,1)}), bf16[32,16,6144]{2,1,0:T(8,128)(2,1)}) %all-gather.2.cloned.1.call-update) | async-done | bytes 6291472 | tf_op jit(solution)/shard_map/all_gather | solution.py:53
  83.4 6.3 %fusion.20 = f32[512,256]{1,0:T(8,128)} fusion(bf16[512,6144]{1,0:T(8,128)(2,1)} %bitcast.33, bf16[6144,256]{1,0:T(8,128)(2,1)} %bitcast_multiply_fusion.2), kind=kOutput, calls=%fused_computation.40 | convolution fusion | flops 1610612736 | bytes 9961472 | tf_op jit(solution)/shard_map/dot_general | solution.py:63
  89.7 13.1 %convolution_convert_fusion = bf16[512,6144]{1,0:T(8,128)(2,1)} fusion(bf16[256,6144]{1,0:T(8,128)(2,1)S(1)} %bitcast_multiply_fusion, bf16[512,6144]{1,0:T(8,128)(2,1)} %bitcast.34, bf16[6144,256]{1,0:T(8,128)(2,1)} %bitcast_multiply_fusion.1, f32[512,256]{1,0:T(8,128)} %fusion.20), kind=kOutput, calls=%fused_computation | convolution fusion | flops 3225157632 | bytes 19398656 | tf_op jit(solution)/shard_map/dot_general | solution.py:66
  102.8 0.0 copy-start.7
  102.8 0.0 reduce-scatter.2.cloned.1.call-update
  102.8 45.3 %reduce-scatter.2.cloned.1.call-done = bf16[32,16,768]{2,1,0:T(8,128)(2,1)} async-done(((bf16[32,16,6144]{2,1,0:T(8,128)(2,1)}), bf16[32,16,768]{2,1,0:T(8,128)(2,1)}) %reduce-scatter.2.cloned.1.call-update) | async-done | bytes 786448 | tf_op jit(solution)/shard_map/reduce_scatter | solution.py:70
  148.1 10.2 %all-to-all-start.1 = ((bf16[32,16,768]{2,1,0:T(8,128)(2,1)}), bf16[32,16,768]{2,1,0:T(8,128)(2,1)S(1)}, u32[]{:S(2)}, u32[]{:S(2)}) async-start(bf16[32,16,768]{2,1,0:T(8,128)(2,1)} %reduce-scatter.2.cloned.1.call-done), calls=%async_computation.2 | async-start | bytes 1572864 | tf_op jit(solution)/shard_map/all_to_all | solution.py:76
  158.3 0.0 copy-done.7
  158.3 21.9 %all-to-all-done.1 = bf16[32,16,768]{2,1,0:T(8,128)(2,1)S(1)} async-done(((bf16[32,16,768]{2,1,0:T(8,128)(2,1)}), bf16[32,16,768]{2,1,0:T(8,128)(2,1)S(1)}, u32[]{:S(2)}, u32[]{:S(2)}) %all-to-all-start.1) | async-done | bytes 786464 | tf_op jit(solution)/shard_map/all_to_all | solution.py:76
  180.2 0.1 convert_reduce_fusion
  180.3 0.8 convolution_convert_fusion.2
  (2 shorter events, 0.0 us)
Async XLA Ops:
  6.5 2.3 %copy-start = (bf16[32,768]{1,0:T(8,128)(2,1)S(1)}, bf16[32,768]{1,0:T(8,128)(2,1)}, u32[]{:S(2)}) copy-start(bf16[32,768]{1,0:T(8,128)(2,1)} %param.9) | copy-start | bytes 147460
  6.5 36.7 %copy-start.1 = (bf16[6144,256]{1,0:T(8,128)(2,1)S(1)}, bf16[6144,256]{1,0:T(8,128)(2,1)}, u32[]{:S(2)}) copy-start(bf16[6144,256]{1,0:T(8,128)(2,1)} %param.12) | copy-start | bytes 9437188
  6.5 36.7 %copy-start.4 = (bf16[192,256]{1,0:T(8,128)(2,1)S(1)}, bf16[192,256]{1,0:T(8,128)(2,1)}, u32[]{:S(2)}) copy-start(bf16[192,256]{1,0:T(8,128)(2,1)} %param.13) | copy-start | bytes 294916
  6.5 76.9 %all-gather.2.cloned.1.call-start = ((), (), s32[]{:S(2)}) async-start(), calls=%async_computation.3 | async-start | bytes 7077888 | tf_op jit(solution)/shard_map/all_gather | solution.py:53
  43.2 2.0 %copy-start.5 = (bf16[8,6144]{1,0:T(8,128)(2,1)S(1)}, bf16[8,6144]{1,0:T(8,128)(2,1)}, u32[]{:S(2)}) copy-start(bf16[8,6144]{1,0:T(8,128)(2,1)} %param.17) | copy-start | bytes 294916
  43.2 104.9 %reduce-scatter.2.cloned.1.call-start = ((), (), s32[]{:S(2)}) async-start(), calls=%async_computation.4 | async-start | bytes 7077888 | tf_op jit(solution)/shard_map/reduce_scatter | solution.py:70
  43.2 3.0 %copy-start.2 = (bf16[256,6144]{1,0:T(8,128)(2,1)S(1)}, bf16[256,6144]{1,0:T(8,128)(2,1)}, u32[]{:S(2)}) copy-start(bf16[256,6144]{1,0:T(8,128)(2,1)} %param.16) | copy-start | bytes 9437188
  46.3 1.9 %copy-start.3 = (bf16[6144,256]{1,0:T(8,128)(2,1)S(1)}, bf16[6144,256]{1,0:T(8,128)(2,1)}, u32[]{:S(2)}) copy-start(bf16[6144,256]{1,0:T(8,128)(2,1)} %param.14) | copy-start | bytes 9437188
  46.3 1.9 %copy-start.6 = (bf16[192,256]{1,0:T(8,128)(2,1)S(1)}, bf16[192,256]{1,0:T(8,128)(2,1)}, u32[]{:S(2)}) copy-start(bf16[192,256]{1,0:T(8,128)(2,1)} %param.15) | copy-start | bytes 294916
  102.8 55.5 %copy-start.7 = (f32[32,2]{0,1:T(2,128)S(1)}, f32[32,2]{0,1:T(2,128)}, u32[]{:S(2)}) copy-start(f32[32,2]{0,1:T(2,128)} %param.11) | copy-start | bytes 772
  148.1 32.1 %all-to-all-start.1 = ((bf16[32,16,768]{2,1,0:T(8,128)(2,1)}), bf16[32,16,768]{2,1,0:T(8,128)(2,1)S(1)}, u32[]{:S(2)}, u32[]{:S(2)}) async-start(bf16[32,16,768]{2,1,0:T(8,128)(2,1)} %reduce-scatter.2.cloned.1.call-done), calls=%async_computation.2 | async-start | bytes 1572864 | tf_op jit(solution)/shard_map/all_to_all | solution.py:76
Sparse Core Ops, SparseCore 0:
  43.3 40.1 all-gather.1
  102.9 45.1 reduce-scatter.1
where the time goes:
time: 188 us
  waiting for transfers between devices  101 us (54%)
  blocking collectives  34.1 us (18%)
  matrix products  20.4 us (11%)
  between operations  13.5 us (7%)
  starting transfers between devices  10.2 us (5%)
  other arithmetic  5.26 us (3%)
  local copies, waits for them, and re-layouts  3.99 us (2%)
    reduce_scatter x1, waiting for transfers between devices, per_device(): lax.psum_scatter(partial_value.astype(jnp.float32).astype(jnp.bfloat16),...  45.3 us
    all_to_all x1, blocking collectives, per_device(): lax.all_to_all(jnp.repeat(packed, owners, axis=0), 'ep', split_axis=0, co...  34.1 us
    all_gather x1, waiting for transfers between devices, per_device(): lax.all_gather(lax.all_to_all(jnp.repeat(packed, owners, axis=0), 'ep', s...  33.4 us
    all_to_all x1, waiting for transfers between devices, per_device(): lax.all_to_all(reduced.astype(jnp.bfloat16), 'ep', split_axis=0, concat_a...  21.9 us
    dot_general x1, matrix products, per_device(): jnp.dot(hidden, down_matrix, preferred_element_type=jnp.float32)  13.1 us
    all_to_all x1, starting transfers between devices, per_device(): lax.all_to_all(reduced.astype(jnp.bfloat16), 'ep', split_axis=0, concat_a...  10.2 us
    dot_general x1, matrix products, per_device(): jnp.dot(flat_rows, gate_matrix, preferred_element_type=jnp.float32)  6.3 us
    mul x3, other arithmetic, dequant(): code_values.reshape(count_in // 32, 32, count_out) * scales[:, None, :]  4.1 us
  transfers between devices with their start and end apart: 3, of which 3 were waited for; matrix products, arithmetic and copies ran while one was open for 2% of the time, Pallas kernels for 0%

commit v1 on v0

--- a/solution.py
+++ b/solution.py
@@ -50,14 +50,12 @@
     chosen = chosen.astype(jnp.bfloat16)
     packed = jnp.dot(chosen, tokens, preferred_element_type=jnp.float32).astype(jnp.bfloat16)
     packed = packed.reshape(EXPERTS, CAP, tokens.shape[1])
-    slot_rows = lax.all_gather(
-        lax.all_to_all(
-            jnp.repeat(packed, owners, axis=0), "ep", split_axis=0, concat_axis=0, tiled=True
-        ),
-        "tp",
-        axis=2,
-        tiled=True,
+    x = lax.all_to_all(
+        jnp.repeat(packed, owners, axis=0), "ep", split_axis=0, concat_axis=0, tiled=True
     )
+    size = lax.axis_size("tp")
+    repeats = [size if d == 2 else 1 for d in range(x.ndim)]
+    slot_rows = lax.all_to_all(jnp.tile(x, repeats), "tp", split_axis=2, concat_axis=2, tiled=True)
     count_src, count_slots, model_width = slot_rows.shape
     flat_rows = slot_rows.reshape(count_src * count_slots, model_width)
     gate_proj = jnp.dot(flat_rows, gate_matrix, preferred_element_type=jnp.float32)

time: 188 us -> 309 us (1.64)
  local copies, waits for them, and re-layouts: 3.99 us -> 91.9 us
  waiting for transfers between devices: 101 us -> 127 us
  starting transfers between devices: 10.2 us -> 15.4 us
    all_to_all x0 -> x1, waiting for transfers between devices: none -> 65.1 us  [per_device(): lax.all_to_all(jnp.tile(x, repeats), 'tp', split_axis=2, concat_axis=2, t...]
    unnamed x17 -> x21, local copies, waits for them, and re-layouts: 3.64 us -> 47 us
    all_to_all x0 -> x2, local copies, waits for them, and re-layouts: none -> 34.2 us  [the longest x1 28.9 us: per_device(): lax.all_to_all(jnp.tile(x, repeats), 'tp', split_axis=2, concat_axis=2, t...]
    all_gather x1 -> x0, waiting for transfers between devices: 33.4 us -> none  [per_device(): lax.all_gather(lax.all_to_all(jnp.repeat(packed, owners, axis=0), 'ep', s...]
    another operation x0 -> x1, local copies, waits for them, and re-layouts: none -> 10.4 us  [per_device(): jnp.tile(x, repeats)]
    reduce_scatter x1, waiting for transfers between devices: 45.3 us -> 40.1 us  [per_device(): lax.psum_scatter(partial_value.astype(jnp.float32).astype(jnp.bfloat16),...]
    all_to_all x0 -> x1, starting transfers between devices: none -> 5.07 us  [per_device(): lax.all_to_all(jnp.tile(x, repeats), 'tp', split_axis=2, concat_axis=2, t...]
  transfers between devices with their start and end apart: 3 -> 3, of which waited for: 3 -> 3; matrix products, arithmetic and copies ran while one was open for 2% -> 1% of each run, Pallas kernels for 0% -> 0%
where the time goes in v1:
time: 309 us; the launch traced here: 308 us
  waiting for transfers between devices  127 us (41%)
  local copies, waits for them, and re-layouts  91.9 us (30%)
  blocking collectives  34.1 us (11%)
  matrix products  20.4 us (7%)
  starting transfers between devices  15.4 us (5%)
  between operations  13.5 us (4%)
  other arithmetic  5.21 us (2%)
    all_to_all x1, waiting for transfers between devices, per_device(): lax.all_to_all(jnp.tile(x, repeats), 'tp', split_axis=2, concat_axis=2, t...  65.1 us
    unnamed x21, local copies, waits for them, and re-layouts  47 us
    reduce_scatter x1, waiting for transfers between devices, per_device(): lax.psum_scatter(partial_value.astype(jnp.float32).astype(jnp.bfloat16),...  40.1 us
    all_to_all x1, blocking collectives, per_device(): lax.all_to_all(jnp.repeat(packed, owners, axis=0), 'ep', split_axis=0, co...  34.1 us
    all_to_all x1, local copies, waits for them, and re-layouts, per_device(): lax.all_to_all(jnp.tile(x, repeats), 'tp', split_axis=2, concat_axis=2, t...  28.9 us
    all_to_all x1, waiting for transfers between devices, per_device(): lax.all_to_all(reduced.astype(jnp.bfloat16), 'ep', split_axis=0, concat_a...  21.9 us
    dot_general x1, matrix products, per_device(): jnp.dot(hidden, down_matrix, preferred_element_type=jnp.float32)  13.1 us
    another operation x1, local copies, waits for them, and re-layouts, per_device(): jnp.tile(x, repeats)  10.4 us
  transfers between devices with their start and end apart: 3, of which 3 were waited for; matrix products, arithmetic and copies ran while one was open for 1% of the time, Pallas kernels for 0%

profile of v1, /device:TPU:8, one launch (start us, length us, event | category | flops | bytes accessed | tf_op | source)
XLA Modules:
  0.0 307.6 jit_solution(10668469831146113696)
XLA Ops:
  6.5 0.0 copy-start
  6.5 0.8 copy.30
  7.3 0.1 eq.59
  7.4 0.1 fusion.9
  7.5 0.1 reduce_window_sum.11
  7.6 0.2 select_reduce_fusion
  7.8 0.1 reduce_sum.21
  7.9 0.1 copy.31
  8.0 0.7 multiply_add_fusion
  8.7 0.0 copy-done
  8.7 0.2 convolution_convert_fusion.1
  8.9 0.1 broadcast_in_dim.2
  8.9 34.1 %all_to_all.15 = bf16[32,16,768]{2,1,0:T(8,128)(2,1)} all-to-all(bf16[32,16,768]{2,1,0:T(8,128)(2,1)S(1)} %bitcast.37), channel_id=1, replica_groups=mesh['ep'=32,'tp'=8] {'ep'}, dimensions={0} | all-to-all | bytes 1572864 | tf_op jit(solution)/shard_map/all_to_all | solution.py:53
  43.0 5.2 %copy.32 = bf16[32,16,768]{0,1,2:T(8,128)(2,1)S(1)} copy(bf16[32,16,768]{2,1,0:T(8,128)(2,1)} %all_to_all.15) | data formatting | bytes 1572864 | tf_op jit(solution)/shard_map/all_to_all | solution.py:53
  48.2 10.4 %tile.4 = bf16[32,16,8,768]{0,1,3,2:T(8,128)(2,1)} broadcast(bf16[32,16,768]{0,1,2:T(8,128)(2,1)S(1)} %copy.32), dimensions={0,1,3} | broadcast | bytes 7077888 | tf_op jit(solution)/shard_map/tile | solution.py:58
  58.6 27.2 %reshape.50 = bf16[8,2,196608]{2,1,0:T(2,128)(2,1)} reshape(bf16[6144,16,32]{2,1,0:T(8,128)(2,1)} %bitcast.32) | data formatting | bytes 12582912
  85.8 0.0 copy-start.2
  85.8 0.0 copy-start.5
  85.8 5.1 %all-to-all-start.1 = ((bf16[8,2,196608]{2,1,0:T(2,128)(2,1)}), bf16[8,2,196608]{2,1,0:T(2,128)(2,1)}, u32[]{:S(2)}, u32[]{:S(2)}) async-start(bf16[8,2,196608]{2,1,0:T(2,128)(2,1)} %reshape.50), calls=%async_computation.1 | async-start | bytes 12582912 | tf_op jit(solution)/shard_map/all_to_all | solution.py:58
  90.8 0.0 copy-start.6
  90.8 0.2 reduce-scatter.2.cloned.1.call-start
  91.1 0.0 copy-done.2
  91.1 0.0 copy-done.5
  91.1 0.0 copy-start.3
  91.1 1.9 bitcast_multiply_fusion.2
  93.0 0.0 copy-done.6
  93.0 1.1 copy-done.3
  94.1 0.0 copy-start.4
  94.1 0.0 copy-start.7
  94.1 0.3 bitcast_multiply_fusion
  94.4 1.6 copy-done.4
  96.0 0.0 copy-done.7
  96.0 1.9 bitcast_multiply_fusion.1
  97.9 65.1 %all-to-all-done.1 = bf16[8,2,196608]{2,1,0:T(2,128)(2,1)} async-done(((bf16[8,2,196608]{2,1,0:T(2,128)(2,1)}), bf16[8,2,196608]{2,1,0:T(2,128)(2,1)}, u32[]{:S(2)}, u32[]{:S(2)}) %all-to-all-start.1) | async-done | bytes 6291488 | tf_op jit(solution)/shard_map/all_to_all | solution.py:58
  162.9 16.3 %reshape.51 = bf16[6144,16,32]{2,1,0:T(8,128)(2,1)} reshape(bf16[8,2,196608]{2,1,0:T(2,128)(2,1)} %all-to-all-done.1) | data formatting | bytes 12582912
  179.3 28.9 %copy.33 = bf16[32,16,6144]{2,1,0:T(8,128)(2,1)} copy(bf16[32,16,6144]{0,1,2:T(8,128)(2,1)} %bitcast.33) | data formatting | bytes 12582912 | tf_op jit(solution)/shard_map/all_to_all | solution.py:58
  208.2 6.3 %fusion.20 = f32[512,256]{1,0:T(8,128)} fusion(bf16[512,6144]{1,0:T(8,128)(2,1)} %bitcast.35, bf16[6144,256]{1,0:T(8,128)(2,1)} %bitcast_multiply_fusion.2), kind=kOutput, calls=%fused_computation.40 | convolution fusion | flops 1610612736 | bytes 9961472 | tf_op jit(solution)/shard_map/dot_general | solution.py:61
  214.5 13.1 %convolution_convert_fusion = bf16[512,6144]{1,0:T(8,128)(2,1)} fusion(bf16[256,6144]{1,0:T(8,128)(2,1)S(1)} %bitcast_multiply_fusion, bf16[512,6144]{1,0:T(8,128)(2,1)} %bitcast.36, bf16[6144,256]{1,0:T(8,128)(2,1)} %bitcast_multiply_fusion.1, f32[512,256]{1,0:T(8,128)} %fusion.20), kind=kOutput, calls=%fused_computation | convolution fusion | flops 3225157632 | bytes 19398656 | tf_op jit(solution)/shard_map/dot_general | solution.py:64
  227.6 0.0 copy-start.1
  227.6 0.0 copy-start.8
  227.6 0.0 reduce-scatter.2.cloned.1.call-update
  227.6 40.1 %reduce-scatter.2.cloned.1.call-done = bf16[32,16,768]{2,1,0:T(8,128)(2,1)} async-done(((bf16[32,16,6144]{2,1,0:T(8,128)(2,1)}), bf16[32,16,768]{2,1,0:T(8,128)(2,1)}) %reduce-scatter.2.cloned.1.call-update) | async-done | bytes 786448 | tf_op jit(solution)/shard_map/reduce_scatter | solution.py:68
  267.7 10.2 %all-to-all-start.2 = ((bf16[32,16,768]{2,1,0:T(8,128)(2,1)}), bf16[32,16,768]{2,1,0:T(8,128)(2,1)S(1)}, u32[]{:S(2)}, u32[]{:S(2)}) async-start(bf16[32,16,768]{2,1,0:T(8,128)(2,1)} %reduce-scatter.2.cloned.1.call-done), calls=%async_computation.3 | async-start | bytes 1572864 | tf_op jit(solution)/shard_map/all_to_all | solution.py:74
  277.8 0.0 copy-done.8
  277.9 21.9 %all-to-all-done.2 = bf16[32,16,768]{2,1,0:T(8,128)(2,1)S(1)} async-done(((bf16[32,16,768]{2,1,0:T(8,128)(2,1)}), bf16[32,16,768]{2,1,0:T(8,128)(2,1)S(1)}, u32[]{:S(2)}, u32[]{:S(2)}) %all-to-all-start.2) | async-done | bytes 786464 | tf_op jit(solution)/shard_map/all_to_all | solution.py:74
  299.8 0.1 convert_reduce_fusion
  299.9 0.8 convolution_convert_fusion.2
  300.7 0.0 copy-done.1
  (2 shorter events, 0.0 us)
Async XLA Ops:
  6.5 2.1 copy-start
  85.8 5.3 %copy-start.2 = (bf16[6144,256]{1,0:T(8,128)(2,1)S(1)}, bf16[6144,256]{1,0:T(8,128)(2,1)}, u32[]{:S(2)}) copy-start(bf16[6144,256]{1,0:T(8,128)(2,1)} %param.12) | copy-start | bytes 9437188
  85.8 5.3 %copy-start.5 = (bf16[192,256]{1,0:T(8,128)(2,1)S(1)}, bf16[192,256]{1,0:T(8,128)(2,1)}, u32[]{:S(2)}) copy-start(bf16[192,256]{1,0:T(8,128)(2,1)} %param.13) | copy-start | bytes 294916
  85.8 77.2 %all-to-all-start.1 = ((bf16[8,2,196608]{2,1,0:T(2,128)(2,1)}), bf16[8,2,196608]{2,1,0:T(2,128)(2,1)}, u32[]{:S(2)}, u32[]{:S(2)}) async-start(bf16[8,2,196608]{2,1,0:T(2,128)(2,1)} %reshape.50), calls=%async_computation.1 | async-start | bytes 12582912 | tf_op jit(solution)/shard_map/all_to_all | solution.py:58
  90.8 2.2 copy-start.6
  90.8 176.8 %reduce-scatter.2.cloned.1.call-start = ((), (), s32[]{:S(2)}) async-start(), calls=%async_computation.4 | async-start | bytes 7077888 | tf_op jit(solution)/shard_map/reduce_scatter | solution.py:68
  91.1 3.0 copy-start.3
  94.1 1.9 copy-start.4
  94.1 1.9 copy-start.7
  227.6 73.1 %copy-start.1 = (bf16[32,768]{1,0:T(8,128)(2,1)S(1)}, bf16[32,768]{1,0:T(8,128)(2,1)}, u32[]{:S(2)}) copy-start(bf16[32,768]{1,0:T(8,128)(2,1)} %param.9) | copy-start | bytes 147460
  227.6 50.3 %copy-start.8 = (f32[32,2]{0,1:T(2,128)S(1)}, f32[32,2]{0,1:T(2,128)}, u32[]{:S(2)}) copy-start(f32[32,2]{0,1:T(2,128)} %param.11) | copy-start | bytes 772
  267.7 32.1 %all-to-all-start.2 = ((bf16[32,16,768]{2,1,0:T(8,128)(2,1)}), bf16[32,16,768]{2,1,0:T(8,128)(2,1)S(1)}, u32[]{:S(2)}, u32[]{:S(2)}) async-start(bf16[32,16,768]{2,1,0:T(8,128)(2,1)} %reduce-scatter.2.cloned.1.call-done), calls=%async_computation.3 | async-start | bytes 1572864 | tf_op jit(solution)/shard_map/all_to_all | solution.py:74
Sparse Core Ops, SparseCore 0:
  227.7 39.8 reduce-scatter.1
